TPU v7x, 256 devices: a whole 4x4x8 slice. The times are simulated.
256 devices in a mesh: ens: 16 (over z, y_hi), mp: 16 (over x, y_lo, core).
Axes of the slice: x: 4, y: 4 (y_hi: 2, y_lo: 2; y = y_hi * 2 + y_lo), z: 8, core: 2. Of those that a mesh axis runs over, the one named last changes fastest.
Arguments:
- tokens: bfloat16 [16, 8192, 1024], P('ens', 'mp'), may hold values from -6 to 6
- ln_gain: float32 [1024], replicated, may hold values from 0.5 to 1.5
- w_qkv: bfloat16 [1024, 3072], replicated, may hold values from -1 to 1
- w_out: bfloat16 [1024, 1024], replicated, may hold values from -0.75 to 0.75
- neighbours: int32 [4, 32768], P(None, 'mp'), may hold values from 0 to 8191, as said below
- edge_weights: float32 [4, 32768], P(None, 'mp'), may hold values from 0.2 to 1
- w_dec: bfloat16 [100, 1024], replicated, may hold values from -0.1875 to 0.1875
- truth: float32 [100, 32768], P(None, ('mp', 'ens')), may hold values from -6 to 6
Outputs:
- crps_score: float32 [100, 32768], P(None, ('mp', 'ens'))
Inputs may be any that keep to these rules, and one draw needn't show every extreme that they name: `neighbours`: the tokens of point g are among tokens g // 2048 * 512 to g // 2048 * 512 + 511 of its member.
All inputs are finite; a program needn't handle non-finite values.
Results may differ from a plain program's by a relative error of at most 0.0028.
The roundings to bfloat16 on the way count: a program that leaves them out, or rounds other values in their place, can miss the bound.
Values may be sent and summed in bfloat16 or wider, within the bound.
A program may use at most 128 MiB of HBM per device.

v0:
```python
import jax
import jax.numpy as jnp
from jax import lax
from jax.sharding import PartitionSpec as P

HEADS = 16
NEIGH = 4
HALF = 512
ALPHA = 0.95


def layer_norm(inputs, ln_gain):
    values = inputs.astype(jnp.float32)
    average = jnp.mean(values, axis=-1, keepdims=True)
    centred = values - average
    variance = jnp.mean(centred * centred, axis=-1, keepdims=True)
    return (centred * lax.rsqrt(variance + 1e-05) * ln_gain).astype(jnp.bfloat16)


def attend(queries, key_rows, value_rows, first_row, seq_tokens):
    count = queries.shape[1]
    head_dim = queries.shape[-1]
    scores = jnp.einsum(
        "mqhe,mkhe->mhqk", queries, key_rows, preferred_element_type=jnp.float32
    ) / jnp.sqrt(jnp.float32(head_dim))
    query_pos = first_row + jnp.arange(count, dtype=jnp.int32)
    key_pos = first_row - HALF + jnp.arange(count + 2 * HALF, dtype=jnp.int32)
    allowed = (
        (key_pos[None, :] >= 0)
        & (key_pos[None, :] < seq_tokens)
        & (jnp.abs(key_pos[None, :] - query_pos[:, None]) <= HALF)
    )
    scores = jnp.where(allowed[None, None], scores, -1e30)
    top = jnp.max(scores, axis=-1, keepdims=True)
    expo = jnp.exp(scores - top)
    weights = (expo / jnp.sum(expo, axis=-1, keepdims=True)).astype(jnp.bfloat16)
    context = jnp.einsum("mhqk,mkhe->mqhe", weights, value_rows, preferred_element_type=jnp.float32)
    return context.astype(jnp.bfloat16)


def shards(tokens, ln_gain, w_qkv, w_out, neighbours, edge_weights, w_dec, truth):
    members_here, tok_rows, model_width = tokens.shape
    lane_count = lax.axis_size("mp")
    lane_index = lax.axis_index("mp")
    seq_tokens = tok_rows * lane_count
    head_count = HEADS
    head_dim = model_width // head_count
    normed = layer_norm(tokens, ln_gain)
    projected = jnp.einsum("mtd,de->mte", normed, w_qkv, preferred_element_type=jnp.float32).astype(
        jnp.bfloat16
    )
    by_head = projected.reshape(members_here, tok_rows, 3, head_count, head_dim)
    regroup = lax.all_to_all(by_head, "mp", split_axis=3, concat_axis=1, tiled=True)
    local_heads = head_count // lane_count
    queries = regroup[:, :, 0]
    key_pad = jnp.pad(regroup[:, :, 1], ((0, 0), (HALF, HALF), (0, 0), (0, 0)))
    value_pad = jnp.pad(regroup[:, :, 2], ((0, 0), (HALF, HALF), (0, 0), (0, 0)))

    def block_attend(block_index):
        first_row = block_index * tok_rows
        query_block = lax.dynamic_slice_in_dim(queries, first_row, tok_rows, 1)
        key_block = lax.dynamic_slice_in_dim(key_pad, first_row, tok_rows + 2 * HALF, 1)
        value_block = lax.dynamic_slice_in_dim(value_pad, first_row, tok_rows + 2 * HALF, 1)
        return attend(query_block, key_block, value_block, first_row, seq_tokens)

    block_outs = lax.map(block_attend, jnp.arange(lane_count, dtype=jnp.int32))
    all_rows = jnp.moveaxis(block_outs, 0, 1).reshape(
        members_here, seq_tokens, local_heads, head_dim
    )
    context = lax.all_to_all(all_rows, "mp", split_axis=1, concat_axis=2, tiled=True)
    context = context.reshape(members_here, tok_rows, model_width)
    proj_out = jnp.einsum("mtd,de->mte", context, w_out, preferred_element_type=jnp.float32)
    processed = (tokens.astype(jnp.float32) + proj_out).astype(jnp.bfloat16)
    local_index = neighbours - lane_index * tok_rows
    hidden = jnp.zeros((members_here, neighbours.shape[1], model_width), jnp.float32)
    for slot_index in range(NEIGH):
        picked = jnp.take(processed, local_index[slot_index], axis=1)
        hidden = hidden + edge_weights[slot_index][None, :, None] * picked.astype(jnp.float32)
    decoded = jnp.einsum(
        "vd,mgd->mvg", w_dec, hidden.astype(jnp.bfloat16), preferred_element_type=jnp.float32
    ).astype(jnp.bfloat16)
    gathered = lax.all_to_all(decoded, "ens", split_axis=2, concat_axis=0, tiled=True).astype(
        jnp.float32
    )
    member_total = gathered.shape[0]
    skill_term = jnp.mean(jnp.abs(gathered - truth[None]), axis=0)
    spread = jnp.sum(jnp.abs(gathered[:, None] - gathered[None, :]), axis=(0, 1))
    coeff = ALPHA / (2.0 * member_total * (member_total - 1)) + (1.0 - ALPHA) / (
        2.0 * member_total * member_total
    )
    return skill_term - coeff * spread


def solution(mesh):
    in_specs = (
        P("ens", "mp", None),
        P(),
        P(),
        P(),
        P(None, "mp"),
        P(None, "mp"),
        P(),
        P(None, ("mp", "ens")),
    )
    out_specs = P(None, ("mp", "ens"))
    return jax.shard_map(shards, mesh=mesh, in_specs=in_specs, out_specs=out_specs, check_vma=False)
```

profile of v0, /device:TPU:8, one launch (start us, length us, event | category | flops | bytes accessed | tf_op | source)
XLA Modules:
  0.0 371.9 jit_solution(4626940275149164872)
XLA Ops:
  0.0 1.6 convert_reduce_fusion
  1.6 1.6 fusion.26
  3.2 8.3 %convolution_convert_fusion = bf16[512,3072]{1,0:T(8,128)(2,1)} fusion(bf16[1024,3072]{1,0:T(8,128)(2,1)} %param.14, bf16[1,512,1024]{2,1,0:T(8,128)(2,1)} %param.12, f32[1024]{0:T(1024)} %param.13, f32[512]{0:T(512)S(1)} %add_rsqrt_fusion, f32[512]{0:T(512)S(1)} %broadcast_multiply_fusion), kind=kOutput, calls=%fused_computation.28 | convolution fusion | flops 3225419776 | bytes 10493952 | tf_op jit(solution)/shard_map/mtd,de->mte/dot_general | solution.py:49
  11.5 4.7 %copy.45 = bf16[512,3072]{0,1:T(8,128)(2,1)} copy(bf16[512,3072]{1,0:T(8,128)(2,1)} %convolution_convert_fusion) | data formatting | bytes 6291456 | tf_op jit(solution)/shard_map/convert_element_type | solution.py:49
  16.2 3.9 %copy.46 = bf16[1,512,3,16,64]{1,4,2,0,3:T(8,128)(2,1)} copy(bf16[1,512,3,16,64]{1,4,3,2,0:T(8,128)(2,1)} %bitcast.144) | data formatting | bytes 6291456 | tf_op jit(solution)/shard_map/reshape | solution.py:52
  20.2 6.5 %all-to-all-start = ((bf16[1,512,3,16,64]{1,4,2,0,3:T(8,128)(2,1)}), bf16[1,512,3,16,64]{1,4,2,0,3:T(8,128)(2,1)}, u32[]{:S(2)}, u32[]{:S(2)}) async-start(bf16[1,512,3,16,64]{1,4,2,0,3:T(8,128)(2,1)} %copy.46), calls=%async_computation | async-start | bytes 6291456 | tf_op jit(solution)/shard_map/all_to_all | solution.py:53
  26.8 42.5 %all-to-all-done = bf16[1,512,3,16,64]{1,4,2,0,3:T(8,128)(2,1)} async-done(((bf16[1,512,3,16,64]{1,4,2,0,3:T(8,128)(2,1)}), bf16[1,512,3,16,64]{1,4,2,0,3:T(8,128)(2,1)}, u32[]{:S(2)}, u32[]{:S(2)}) %all-to-all-start) | async-done | bytes 3145760 | tf_op jit(solution)/shard_map/all_to_all | solution.py:53
  69.3 2.3 copy.57
  71.6 1.3 slice_bitcast_fusion
  73.1 1.1 pad.8
  74.2 92.6 %while.12 = (s32[]{:T(128)}, bf16[16,1,512,1,64]{2,4,3,1,0:T(8,128)(2,1)}, s32[16]{0:T(128)S(1)}, bf16[1,9216,1,64]{1,3,2,0:T(8,128)(2,1)S(1)}, bf16[1,8192,1,64...) while((s32[]{:T(128)}, ...), condition=%wide.region_5.6_spmd, body=%wide.region_2.5_spmd.sunk | while | flops 210803712 | bytes 9991916 | solution.py:66
  75.5 2.4 fusion.54
  78.5 1.5 fusion.56
  81.3 2.4 fusion.54
  84.3 1.5 fusion.56
  87.1 2.4 fusion.54
  90.1 1.4 fusion.56
  92.9 2.4 fusion.54
  95.8 1.5 fusion.56
  98.7 2.4 fusion.54
  101.6 1.4 fusion.56
  104.5 2.4 fusion.54
  107.4 1.5 fusion.56
  110.2 2.4 fusion.54
  113.2 1.5 fusion.56
  116.0 2.4 fusion.54
  119.0 1.5 fusion.56
  121.8 2.4 fusion.54
  124.8 1.5 fusion.56
  127.6 2.4 fusion.54
  130.6 1.5 fusion.56
  133.4 2.4 fusion.54
  136.3 1.5 fusion.56
  139.2 2.4 fusion.54
  142.1 1.4 fusion.56
  145.0 2.4 fusion.54
  147.9 1.4 fusion.56
  150.7 2.4 fusion.54
  153.7 1.5 fusion.56
  156.5 2.4 fusion.54
  159.5 1.5 fusion.56
  162.3 2.4 fusion.54
  165.3 1.5 fusion.56
  166.7 2.8 copy.55
  169.5 12.5 %reshape.226 = bf16[1,8192,1,64]{3,2,0,1:T(2,128)(2,1)} reshape(bf16[16,1,512,1,64]{4,2,0,3,1:T(8,128)(2,1)} %copy.55) | data formatting | bytes 2097152 | tf_op jit(solution)/shard_map/reshape;transpose | solution.py:67
  182.5 46.5 %reduce.12 = bf16[8192,64]{1,0:T(8,128)(2,1)} reduce(bf16[8192,1,1,64]{3,2,1,0:T(2,128)(2,1)} %bitcast.139, bf16[]{:T(256)} %broadcast.155), dimensions={1,2}, to_apply=%bitcast.116.reduce_sub_computation | reduce | bytes 2097154
  229.0 4.7 %reshape.227 = bf16[16,2,16384]{2,1,0:T(2,128)(2,1)} reshape(bf16[8192,64]{1,0:T(8,128)(2,1)} %reduce.12) | data formatting | bytes 2097152
  233.7 4.4 %all-to-all-start.1 = ((bf16[16,2,16384]{2,1,0:T(2,128)(2,1)}), bf16[16,2,16384]{2,1,0:T(2,128)(2,1)S(1)}, u32[]{:S(2)}, u32[]{:S(2)}) async-start(bf16[16,2,16384]{2,1,0:T(2,128)(2,1)} %reshape.227), calls=%async_computation.1 | async-start | bytes 2097152 | tf_op jit(solution)/shard_map/all_to_all | solution.py:70
  238.1 14.8 %all-to-all-done.1 = bf16[16,2,16384]{2,1,0:T(2,128)(2,1)S(1)} async-done(((bf16[16,2,16384]{2,1,0:T(2,128)(2,1)}), bf16[16,2,16384]{2,1,0:T(2,128)(2,1)S(1)}, u32[]{:S(2)}, u32[]{:S(2)}) %all-to-all-start.1) | async-done | bytes 1048608 | tf_op jit(solution)/shard_map/all_to_all | solution.py:70
  252.9 7.0 %reshape.228 = bf16[8192,1,1,64]{3,2,1,0:T(2,128)(2,1)} reshape(bf16[16,2,16384]{2,1,0:T(2,128)(2,1)S(1)} %all-to-all-done.1) | data formatting | bytes 2097152
  259.9 8.2 %copy.50 = bf16[1,8192,1,64]{1,3,2,0:T(8,128)(2,1)S(1)} copy(bf16[1,8192,1,64]{3,2,0,1:T(2,128)(2,1)} %bitcast.138) | data formatting | bytes 2097152 | tf_op jit(solution)/shard_map/all_to_all | solution.py:70
  269.3 1.3 fusion.31
  270.6 9.6 %gather_fusion = bf16[2048,1024]{1,0:T(8,128)(2,1)} fusion(bf16[512,1024]{1,0:T(8,128)(2,1)S(1)} %fusion.31, s32[2048]{0:T(1024)S(1)} %fusion.37), kind=kCustom, calls=%fused_computation.clone | custom fusion | bytes 8396800 | tf_op jit(solution)/shard_map/jit(_take)/gather | solution.py:77
  280.3 9.7 %gather_fusion.1 = bf16[2048,1024]{1,0:T(8,128)(2,1)} fusion(bf16[512,1024]{1,0:T(8,128)(2,1)S(1)} %fusion.31, s32[2048]{0:T(1024)S(1)} %fusion.38), kind=kCustom, calls=%fused_computation.1.clone | custom fusion | bytes 8396800 | tf_op jit(solution)/shard_map/jit(_take)/gather | solution.py:77
  289.9 9.7 %gather_fusion.2 = bf16[2048,1024]{1,0:T(8,128)(2,1)} fusion(bf16[512,1024]{1,0:T(8,128)(2,1)S(1)} %fusion.31, s32[2048]{0:T(1024)S(1)} %fusion.39), kind=kCustom, calls=%fused_computation.2.clone | custom fusion | bytes 8396800 | tf_op jit(solution)/shard_map/jit(_take)/gather | solution.py:77
  299.6 9.7 %gather_fusion.3 = bf16[2048,1024]{1,0:T(8,128)(2,1)} fusion(bf16[512,1024]{1,0:T(8,128)(2,1)S(1)} %fusion.31, s32[2048]{0:T(1024)S(1)} %fusion.40), kind=kCustom, calls=%fused_computation.3.clone | custom fusion | bytes 8396800 | tf_op jit(solution)/shard_map/jit(_take)/gather | solution.py:77
  309.3 9.7 %fusion.23 = bf16[1,100,2048]{2,1,0:T(8,128)(2,1)S(1)} fusion(bf16[100,1024]{1,0:T(8,128)(2,1)S(1)} %copy-done.6, bf16[2048,1024]{1,0:T(8,128)(2,1)} %gather_fusion.3, bf16[2048,1024]{1,0:T(8,128)(2,1)} %gather_fusion.2, bf16[2048,1024]{1,0:T(8,128)(2,1)} %gather_fusion.1, bf16[2048,1024]{1,0:T(8,128)(2,1)} %gather_fusion, f32[2048]{0:T(1024)S(1)} %bitcast.160, ...), kind=kOutput, calls=%fused_computation.41 | convolution fusion | flops 453189632 | bytes 17432576 | tf_op jit(solution)/shard_map/vd,mgd->mvg/dot_general | solution.py:79
  319.7 11.8 %reduce.13 = bf16[2048,100]{1,0:T(8,128)(2,1)S(1)} reduce(bf16[2048,1,100]{2,1,0:T(2,128)(2,1)S(1)} %bitcast.147, bf16[]{:T(256)} %broadcast.155), dimensions={1}, to_apply=%bitcast.118.reduce_sub_computation | reduce | bytes 819202
  331.5 1.7 reshape.229
  333.2 27.9 %all_to_all.42 = bf16[16,2,6400]{2,1,0:T(2,128)(2,1)S(1)} all-to-all(bf16[16,2,6400]{2,1,0:T(2,128)(2,1)S(1)} %reshape.229), channel_id=1, replica_groups=mesh['ens'=16,'mp'=16] {'ens'}, dimensions={0} | all-to-all | bytes 819200 | tf_op jit(solution)/shard_map/all_to_all | solution.py:82
  361.1 2.2 reshape.230
  363.3 3.8 %copy.53 = bf16[1,100,2048]{2,0,1:T(2,128)(2,1)} copy(bf16[1,100,2048]{1,0,2:T(2,128)(2,1)S(1)} %bitcast.146) | data formatting | bytes 819200 | tf_op jit(solution)/shard_map/all_to_all | solution.py:82
  367.1 2.0 convert_element_type.97
  369.4 1.6 abs_reduce_fusion
  (115 shorter events, 23.8 us)
Async XLA Ops:
  0.0 269.0 %copy-start = (bf16[1024,1024]{1,0:T(8,128)(2,1)S(1)}, bf16[1024,1024]{1,0:T(8,128)(2,1)}, u32[]{:S(2)}) copy-start(bf16[1024,1024]{1,0:T(8,128)(2,1)} %param.15) | copy-start | bytes 6291460
  20.2 6.5 %copy-start.4 = (s32[4,2048]{1,0:T(4,128)S(1)}, s32[4,2048]{1,0:T(4,128)}, u32[]{:S(2)}) copy-start(s32[4,2048]{1,0:T(4,128)} %param.16) | copy-start | bytes 98308
  20.2 49.2 %all-to-all-start = ((bf16[1,512,3,16,64]{1,4,2,0,3:T(8,128)(2,1)}), bf16[1,512,3,16,64]{1,4,2,0,3:T(8,128)(2,1)}, u32[]{:S(2)}, u32[]{:S(2)}) async-start(bf16[1,512,3,16,64]{1,4,2,0,3:T(8,128)(2,1)} %copy.46), calls=%async_computation | async-start | bytes 6291456 | tf_op jit(solution)/shard_map/all_to_all | solution.py:53
  229.0 9.1 %copy-start.5 = (f32[4,2048]{1,0:T(4,128)S(1)}, f32[4,2048]{1,0:T(4,128)}, u32[]{:S(2)}) copy-start(f32[4,2048]{1,0:T(4,128)} %param.17) | copy-start | bytes 98308
  233.7 19.2 %all-to-all-start.1 = ((bf16[16,2,16384]{2,1,0:T(2,128)(2,1)}), bf16[16,2,16384]{2,1,0:T(2,128)(2,1)S(1)}, u32[]{:S(2)}, u32[]{:S(2)}) async-start(bf16[16,2,16384]{2,1,0:T(2,128)(2,1)} %reshape.227), calls=%async_computation.1 | async-start | bytes 2097152 | tf_op jit(solution)/shard_map/all_to_all | solution.py:70
  268.1 1.2 copy-start.2
  299.6 9.7 %copy-start.6 = (bf16[100,1024]{1,0:T(8,128)(2,1)S(1)}, bf16[100,1024]{1,0:T(8,128)(2,1)}, u32[]{:S(2)}) copy-start(bf16[100,1024]{1,0:T(8,128)(2,1)} %param.18) | copy-start | bytes 614404
  363.3 7.7 %copy-start.3 = (f32[100,128]{1,0:T(8,128)S(1)}, f32[100,128]{1,0:T(8,128)}, u32[]{:S(2)}) copy-start(f32[100,128]{1,0:T(8,128)} %param.19) | copy-start | bytes 153604
  363.3 8.6 %copy-start.1 = (bf16[1024,1024]{1,0:T(8,128)(2,1)S(1)}, bf16[1024,1024]{1,0:T(8,128)(2,1)}, u32[]{:S(2)}) copy-start(bf16[1024,1024]{1,0:T(8,128)(2,1)} %param.15) | copy-start | bytes 6291460
where the time goes:
time: 374 us; the launch traced here: 372 us
  local copies, waits for them, and re-layouts  108 us (29%)
  matrix products  80.5 us (22%)
  other arithmetic  75.6 us (20%)
  waiting for transfers between devices  57.3 us (15%)
  blocking collectives  27.9 us (7%)
  loops' own time  11.5 us (3%)
  starting transfers between devices  10.9 us (3%)
    unnamed x2, other arithmetic  58.3 us
    all_to_all x1, waiting for transfers between devices, shards(): lax.all_to_all(by_head, 'mp', split_axis=3, concat_axis=1, tiled=True)  42.5 us
    gather x4, local copies, waits for them, and re-layouts, shards(): picked = jnp.take(processed, local_index[slot_index], axis=1)  38.6 us
    dot_general x16, matrix products, attend(): jnp.einsum('mqhe,mkhe->mhqk', queries, key_rows, preferred_element_type=j...  38 us
    all_to_all x1, blocking collectives, shards(): lax.all_to_all(decoded, 'ens', split_axis=2, concat_axis=0, tiled=True)  27.9 us
    dot_general x16, matrix products, attend(): jnp.einsum('mhqk,mkhe->mqhe', weights, value_rows, preferred_element_type...  23.2 us
    unnamed x20, local copies, waits for them, and re-layouts  16.7 us
    another operation x2, local copies, waits for them, and re-layouts, shards(): jnp.moveaxis(block_outs, 0, 1)  15.3 us
  transfers between devices with their start and end apart: 2, of which 2 were waited for; matrix products, arithmetic and copies ran while one was open for 0% of the time, Pallas kernels for 0%

commit v1 on v0

--- a/solution.py
+++ b/solution.py
@@ -67,7 +67,10 @@
     all_rows = jnp.moveaxis(block_outs, 0, 1).reshape(
         members_here, seq_tokens, local_heads, head_dim
     )
-    context = lax.all_to_all(all_rows, "mp", split_axis=1, concat_axis=2, tiled=True)
+    context = jnp.concatenate(
+        lax.all_to_all(jnp.stack(jnp.split(all_rows, lax.axis_size("mp"), axis=1)), "mp", 0, 0),
+        axis=2,
+    )
     context = context.reshape(members_here, tok_rows, model_width)
     proj_out = jnp.einsum("mtd,de->mte", context, w_out, preferred_element_type=jnp.float32)
     processed = (tokens.astype(jnp.float32) + proj_out).astype(jnp.bfloat16)

time: 374 us -> 308 us (0.82)
  other arithmetic: 75.6 us -> 29.6 us
  local copies, waits for them, and re-layouts: 108 us -> 86.5 us
    unnamed x2 -> x1, other arithmetic: 58.3 us -> 12.3 us
    another operation x2 -> x1, local copies, waits for them, and re-layouts: 15.3 us -> 1.32 us  [shards(): jnp.moveaxis(block_outs, 0, 1)]
    all_to_all x2 -> x0, local copies, waits for them, and re-layouts: 8.74 us -> none  [shards(): lax.all_to_all(all_rows, 'mp', split_axis=1, concat_axis=2, tiled=True)]
    unnamed x20 -> x30, local copies, waits for them, and re-layouts: 16.7 us -> 15.6 us
where the time goes in v1:
time: 308 us; the launch traced here: 307 us
  local copies, waits for them, and re-layouts  86.5 us (28%)
  matrix products  82.8 us (27%)
  waiting for transfers between devices  57.3 us (19%)
  other arithmetic  29.6 us (10%)
  blocking collectives  27.4 us (9%)
  loops' own time  11.5 us (4%)
  starting transfers between devices  11.4 us (4%)
    all_to_all x1, waiting for transfers between devices, shards(): lax.all_to_all(by_head, 'mp', split_axis=3, concat_axis=1, tiled=True)  42.5 us
    gather x4, local copies, waits for them, and re-layouts, shards(): picked = jnp.take(processed, local_index[slot_index], axis=1)  38.6 us
    dot_general x16, matrix products, attend(): jnp.einsum('mqhe,mkhe->mhqk', queries, key_rows, preferred_element_type=j...  38 us
    all_to_all x1, blocking collectives, shards(): lax.all_to_all(decoded, 'ens', split_axis=2, concat_axis=0, tiled=True)  27.4 us
    dot_general x16, matrix products, attend(): jnp.einsum('mhqk,mkhe->mqhe', weights, value_rows, preferred_element_type...  23.2 us
    unnamed x30, local copies, waits for them, and re-layouts  15.6 us
    all_to_all x1, waiting for transfers between devices, shards(): lax.all_to_all(jnp.stack(jnp.split(all_rows, lax.axis_size('mp'), axis=1)...  14.8 us
    unnamed x1, other arithmetic  12.3 us
  transfers between devices with their start and end apart: 2, of which 2 were waited for; matrix products, arithmetic and copies ran while one was open for 0% of the time, Pallas kernels for 0%

profile of v1, /device:TPU:8, one launch (start us, length us, event | category | flops | bytes accessed | tf_op | source)
XLA Modules:
  0.0 306.5 jit_solution(17100917207828871414)
XLA Ops:
  0.0 1.6 convert_reduce_fusion
  1.6 1.6 fusion.26
  3.2 8.3 %convolution_convert_fusion = bf16[512,3072]{1,0:T(8,128)(2,1)} fusion(bf16[1024,3072]{1,0:T(8,128)(2,1)} %param.14, bf16[1,512,1024]{2,1,0:T(8,128)(2,1)} %param.12, f32[1024]{0:T(1024)} %param.13, f32[512]{0:T(512)S(1)} %add_rsqrt_fusion, f32[512]{0:T(512)S(1)} %broadcast_multiply_fusion), kind=kOutput, calls=%fused_computation.28 | convolution fusion | flops 3225419776 | bytes 10493952 | tf_op jit(solution)/shard_map/mtd,de->mte/dot_general | solution.py:49
  11.5 4.7 %copy.52 = bf16[512,3072]{0,1:T(8,128)(2,1)} copy(bf16[512,3072]{1,0:T(8,128)(2,1)} %convolution_convert_fusion) | data formatting | bytes 6291456 | tf_op jit(solution)/shard_map/convert_element_type | solution.py:49
  16.2 3.9 %copy.53 = bf16[1,512,3,16,64]{1,4,2,0,3:T(8,128)(2,1)} copy(bf16[1,512,3,16,64]{1,4,3,2,0:T(8,128)(2,1)} %bitcast.195) | data formatting | bytes 6291456 | tf_op jit(solution)/shard_map/reshape | solution.py:52
  20.2 6.5 %all-to-all-start = ((bf16[1,512,3,16,64]{1,4,2,0,3:T(8,128)(2,1)}), bf16[1,512,3,16,64]{1,4,2,0,3:T(8,128)(2,1)}, u32[]{:S(2)}, u32[]{:S(2)}) async-start(bf16[1,512,3,16,64]{1,4,2,0,3:T(8,128)(2,1)} %copy.53), calls=%async_computation | async-start | bytes 6291456 | tf_op jit(solution)/shard_map/all_to_all | solution.py:53
  26.8 42.5 %all-to-all-done = bf16[1,512,3,16,64]{1,4,2,0,3:T(8,128)(2,1)} async-done(((bf16[1,512,3,16,64]{1,4,2,0,3:T(8,128)(2,1)}), bf16[1,512,3,16,64]{1,4,2,0,3:T(8,128)(2,1)}, u32[]{:S(2)}, u32[]{:S(2)}) %all-to-all-start) | async-done | bytes 3145760 | tf_op jit(solution)/shard_map/all_to_all | solution.py:53
  69.3 2.3 copy.59
  71.6 1.3 slice_bitcast_fusion
  73.0 1.1 pad.8
  74.1 92.6 %while.12 = (s32[]{:T(128)}, bf16[16,1,512,1,64]{2,4,3,1,0:T(8,128)(2,1)}, s32[16]{0:T(128)S(1)}, bf16[1,9216,1,64]{1,3,2,0:T(8,128)(2,1)S(1)}, bf16[1,8192,1,64...) while((s32[]{:T(128)}, ...), condition=%wide.region_5.6_spmd, body=%wide.region_2.5_spmd.sunk | while | flops 210803712 | bytes 9991916 | solution.py:66
  74.1 0.7 dynamic_slice.48
  75.5 2.4 fusion.70
  78.5 1.5 fusion.72
  81.3 2.4 fusion.70
  84.2 1.5 fusion.72
  85.7 0.6 dynamic_slice.48
  87.1 2.4 fusion.70
  90.0 1.4 fusion.72
  91.5 0.6 dynamic_slice.48
  92.9 2.4 fusion.70
  95.8 1.5 fusion.72
  98.6 2.4 fusion.70
  101.6 1.4 fusion.72
  104.4 2.4 fusion.70
  107.4 1.5 fusion.72
  110.2 2.4 fusion.70
  113.2 1.5 fusion.72
  116.0 2.4 fusion.70
  119.0 1.5 fusion.72
  121.8 2.4 fusion.70
  124.7 1.5 fusion.72
  127.6 2.4 fusion.70
  130.5 1.5 fusion.72
  133.4 2.4 fusion.70
  136.3 1.5 fusion.72
  139.1 2.4 fusion.70
  142.1 1.4 fusion.72
  144.9 2.4 fusion.70
  147.9 1.4 fusion.72
  150.7 2.4 fusion.70
  153.7 1.5 fusion.72
  156.5 2.4 fusion.70
  159.5 1.5 fusion.72
  162.3 2.4 fusion.70
  165.2 1.5 fusion.72
  166.7 1.3 copy.60
  178.0 4.9 %all-to-all-start.1 = ((bf16[16,1,512,1,64]{2,4,3,1,0:T(8,128)(2,1)}), bf16[16,1,512,1,64]{2,4,3,1,0:T(8,128)(2,1)S(1)}, u32[]{:S(2)}, u32[]{:S(2)}) async-start(bf16[16,1,512,1,64]{2,4,3,1,0:T(8,128)(2,1)} %fusion.37), calls=%async_computation.1 | async-start | bytes 2097152 | tf_op jit(solution)/shard_map/all_to_all | solution.py:71
  183.0 14.8 %all-to-all-done.1 = bf16[16,1,512,1,64]{2,4,3,1,0:T(8,128)(2,1)S(1)} async-done(((bf16[16,1,512,1,64]{2,4,3,1,0:T(8,128)(2,1)}), bf16[16,1,512,1,64]{2,4,3,1,0:T(8,128)(2,1)S(1)}, u32[]{:S(2)}, u32[]{:S(2)}) %all-to-all-start.1) | async-done | bytes 1048608 | tf_op jit(solution)/shard_map/all_to_all | solution.py:71
  197.7 1.0 copy-done.1
  198.7 2.8 fusion.31
  201.5 9.6 %gather_fusion = bf16[2048,1024]{1,0:T(8,128)(2,1)} fusion(bf16[512,1024]{1,0:T(8,128)(2,1)S(1)} %fusion.31, s32[2048]{0:T(1024)S(1)} %get-tuple-element.115), kind=kCustom, calls=%fused_computation.clone | custom fusion | bytes 8396800 | tf_op jit(solution)/shard_map/jit(_take)/gather | solution.py:80
  211.2 9.7 %gather_fusion.1 = bf16[2048,1024]{1,0:T(8,128)(2,1)} fusion(bf16[512,1024]{1,0:T(8,128)(2,1)S(1)} %fusion.31, s32[2048]{0:T(1024)S(1)} %get-tuple-element.116), kind=kCustom, calls=%fused_computation.1.clone | custom fusion | bytes 8396800 | tf_op jit(solution)/shard_map/jit(_take)/gather | solution.py:80
  220.9 9.7 %gather_fusion.2 = bf16[2048,1024]{1,0:T(8,128)(2,1)} fusion(bf16[512,1024]{1,0:T(8,128)(2,1)S(1)} %fusion.31, s32[2048]{0:T(1024)S(1)} %get-tuple-element.117), kind=kCustom, calls=%fused_computation.2.clone | custom fusion | bytes 8396800 | tf_op jit(solution)/shard_map/jit(_take)/gather | solution.py:80
  230.5 9.7 %gather_fusion.3 = bf16[2048,1024]{1,0:T(8,128)(2,1)} fusion(bf16[512,1024]{1,0:T(8,128)(2,1)S(1)} %fusion.31, s32[2048]{0:T(1024)S(1)} %get-tuple-element.118), kind=kCustom, calls=%fused_computation.3.clone | custom fusion | bytes 8396800 | tf_op jit(solution)/shard_map/jit(_take)/gather | solution.py:80
  240.2 10.4 %fusion.23 = bf16[1,100,2048]{2,1,0:T(8,128)(2,1)} fusion(bf16[100,1024]{1,0:T(8,128)(2,1)S(1)} %copy-done.5, bf16[2048,1024]{1,0:T(8,128)(2,1)} %gather_fusion.3, bf16[2048,1024]{1,0:T(8,128)(2,1)} %gather_fusion.2, bf16[2048,1024]{1,0:T(8,128)(2,1)} %gather_fusion.1, bf16[2048,1024]{1,0:T(8,128)(2,1)} %gather_fusion, f32[2048]{0:T(1024)S(1)} %bitcast.225, ...), kind=kOutput, calls=%fused_computation.41 | convolution fusion | flops 453189632 | bytes 17432576 | tf_op jit(solution)/shard_map/vd,mgd->mvg/dot_general | solution.py:82
  250.6 2.3 copy.56
  253.5 12.3 %reduce.12 = bf16[2048,100]{1,0:T(8,128)(2,1)} reduce(bf16[2048,1,100]{2,1,0:T(2,128)(2,1)S(1)} %bitcast.213, bf16[]{:T(256)} %broadcast.155), dimensions={1}, to_apply=%bitcast.171.reduce_sub_computation | reduce | bytes 819202
  265.8 2.6 reshape.228
  268.3 27.4 %all_to_all.32 = bf16[16,2,6400]{2,1,0:T(2,128)(2,1)S(1)} all-to-all(bf16[16,2,6400]{2,1,0:T(2,128)(2,1)S(1)} %reshape.228), channel_id=1, replica_groups=mesh['ens'=16,'mp'=16] {'ens'}, dimensions={0} | all-to-all | bytes 819200 | tf_op jit(solution)/shard_map/all_to_all | solution.py:85
  295.8 2.2 reshape.229
  298.0 3.8 %copy.57 = bf16[1,100,2048]{2,0,1:T(2,128)(2,1)} copy(bf16[1,100,2048]{1,0,2:T(2,128)(2,1)S(1)} %bitcast.212) | data formatting | bytes 819200 | tf_op jit(solution)/shard_map/all_to_all | solution.py:85
  301.8 2.0 convert_element_type.97
  304.0 1.6 abs_reduce_fusion
  (120 shorter events, 29.8 us)
Async XLA Ops:
  0.0 198.7 %copy-start = (bf16[1024,1024]{1,0:T(8,128)(2,1)S(1)}, bf16[1024,1024]{1,0:T(8,128)(2,1)}, u32[]{:S(2)}) copy-start(bf16[1024,1024]{1,0:T(8,128)(2,1)} %param.15) | copy-start | bytes 6291460
  20.2 6.5 %copy-start.3 = (s32[4,2048]{1,0:T(4,128)S(1)}, s32[4,2048]{1,0:T(4,128)}, u32[]{:S(2)}) copy-start(s32[4,2048]{1,0:T(4,128)} %param.16) | copy-start | bytes 98308
  20.2 49.1 %all-to-all-start = ((bf16[1,512,3,16,64]{1,4,2,0,3:T(8,128)(2,1)}), bf16[1,512,3,16,64]{1,4,2,0,3:T(8,128)(2,1)}, u32[]{:S(2)}, u32[]{:S(2)}) async-start(bf16[1,512,3,16,64]{1,4,2,0,3:T(8,128)(2,1)} %copy.53), calls=%async_computation | async-start | bytes 6291456 | tf_op jit(solution)/shard_map/all_to_all | solution.py:53
  166.7 16.2 %copy-start.4 = (f32[4,2048]{1,0:T(4,128)S(1)}, f32[4,2048]{1,0:T(4,128)}, u32[]{:S(2)}) copy-start(f32[4,2048]{1,0:T(4,128)} %param.17) | copy-start | bytes 98308
  178.0 19.7 %all-to-all-start.1 = ((bf16[16,1,512,1,64]{2,4,3,1,0:T(8,128)(2,1)}), bf16[16,1,512,1,64]{2,4,3,1,0:T(8,128)(2,1)S(1)}, u32[]{:S(2)}, u32[]{:S(2)}) async-start(bf16[16,1,512,1,64]{2,4,3,1,0:T(8,128)(2,1)} %fusion.37), calls=%async_computation.1 | async-start | bytes 2097152 | tf_op jit(solution)/shard_map/all_to_all | solution.py:71
  197.7 1.0 copy-start.1
  230.5 9.7 %copy-start.5 = (bf16[100,1024]{1,0:T(8,128)(2,1)S(1)}, bf16[100,1024]{1,0:T(8,128)(2,1)}, u32[]{:S(2)}) copy-start(bf16[100,1024]{1,0:T(8,128)(2,1)} %param.18) | copy-start | bytes 614404
  298.0 7.7 %copy-start.2 = (f32[100,128]{1,0:T(8,128)S(1)}, f32[100,128]{1,0:T(8,128)}, u32[]{:S(2)}) copy-start(f32[100,128]{1,0:T(8,128)} %param.19) | copy-start | bytes 153604
